TPU v7x, 128 devices: a whole 4x4x4 slice. The times are simulated.
128 devices in a mesh: mem: 8 (over x, core), tile: 16 (over z, y).
Axes of the slice: x: 4, y: 4, z: 4, core: 2. Of those that a mesh axis runs over, the one named last changes fastest.
Arguments:
- members: bfloat16 [16, 137, 8192], P('mem', None, 'tile'), may hold values from -18 to 18
- vertical: bfloat16 [137, 137], replicated, may hold values from 0 to 1, as said below
- jacobian: bfloat16 [2048, 231, 137], P('tile'), may hold values from -0.5 to 0.5
- sketch_bits: int32 [3, 2048, 231], P(None, 'tile'), may hold values from 0 to 1
- test_bits: int32 [3, 2048, 231], P(None, 'tile'), may hold values from 0 to 1
- obs_column: int32 [2048], P('tile'), may hold values from 0 to 8191, as said below
- obs_slot: int32 [2048], P('tile'), may hold values from 0 to 31, as said below
Outputs:
- image_q: float32 [3, 2048, 231], P(None, 'tile')
- image_w: float32 [3, 2048, 231], P(None, 'tile')
- trace_mean: float32 [], replicated
- sketch_rayleigh: float32 [], replicated
Inputs may be any that keep to these rules, and one draw needn't show every extreme that they name: The observations of owner d are rows d * 128 to (d + 1) * 128 - 1; an observation's column lies in tile obs_column // 512. `obs_slot`: among one owner's observations whose columns lie in the same tile the slots are distinct, so at most 32 of them lie in one tile; every owner has exactly 32 observations in some tile. A vertical correlation matrix: symmetric, positive semidefinite, with ones on the diagonal.
All inputs are finite; a program needn't handle non-finite values.
Results may differ from a plain program's by a relative error of at most 0.0053.
Values may be sent and summed in bfloat16 or wider, within the bound.
No kernel may reach another device: no remote copies, remote signals or barrier semaphores. Data moves between devices by JAX's collectives and lax.ppermute only.
A program may use at most 128 MiB of HBM per device.

v0:
```python
import jax
import jax.numpy as jnp
from jax import lax
from jax.sharding import Mesh
from jax.sharding import PartitionSpec as P

CB = 32
K = 3
STEPS = 6
TILE = ("tile_0", "tile_1")
diffusion_rate = 0.2
highest = lax.Precision.HIGHEST


def with_halo(block, sides, width):
    for axis, dim in sides:
        count = lax.axis_size(axis)
        forward = [(i, i + 1) for i in range(count - 1)]
        forward.append((count - 1, 0))
        backward = [(target, source) for source, target in forward]
        low = lax.ppermute(
            lax.slice_in_dim(block, block.shape[dim] - width, None, axis=dim), axis, forward
        )
        high = lax.ppermute(lax.slice_in_dim(block, 0, width, axis=dim), axis, backward)
        block = jnp.concatenate([low, block, high], axis=dim)
    return block


def gather_turned(arrays, axis, dims):
    turned = [jnp.moveaxis(a, dim, 0) for a, dim in zip(arrays, dims)]
    widths = [t[0].size for t in turned]
    both = jnp.concatenate([t.reshape(-1, w) for t, w in zip(turned, widths)], axis=1)
    whole = lax.all_gather(both, axis, axis=0, tiled=True)
    pieces = jnp.split(whole, [sum(widths[:k]) for k in range(1, len(widths))], axis=1)
    return tuple(
        (
            jnp.moveaxis(b.reshape(-1, *t.shape[1:]), 0, dim)
            for b, t, dim in zip(pieces, turned, dims)
        )
    )


def split_up(value, dim, peers):
    before, after = (value.shape[:dim], value.shape[dim + 1 :])
    return jnp.moveaxis(value.reshape(*before, peers, -1, *after), dim, 0)


def sum_at_owner(value, axis, dim):
    pieces = split_up(value, dim, lax.axis_size(axis))
    arrived = lax.all_to_all(pieces, axis, split_axis=0, concat_axis=0, tiled=True)
    return arrived.sum(axis=0)


def from_everyone(value, axis):
    peers = lax.axis_size(axis)
    return lax.all_to_all(
        jnp.broadcast_to(value[None], (peers, *value.shape)), axis, 0, 0, tiled=True
    )


def joined_along(pieces, dim):
    lengths = list(pieces.shape[1:])
    lengths[dim] *= pieces.shape[0]
    return jnp.moveaxis(pieces, 0, dim).reshape(lengths)


def collect_2(value, axis, dim):
    pieces = from_everyone(value, axis)
    return joined_along(pieces, dim)


def by_axis(value, axes):
    for axis in axes:
        value = lax.psum(value, axis)
    return value


def relax(extended):
    length = extended.shape[-1] - 2 * CB
    center = extended[..., CB : CB + length]
    places = jnp.arange(length) % CB
    west_ok = (places > 0).astype(jnp.float32)
    east_ok = (places < CB - 1).astype(jnp.float32)
    north = extended[..., :length]
    south = extended[..., 2 * CB :]
    west = extended[..., CB - 1 : CB - 1 + length]
    east = extended[..., CB + 1 : CB + 1 + length]
    return center + diffusion_rate * (
        north - center + (south - center) + west_ok * (west - center) + east_ok * (east - center)
    )


def diffuse(state):
    extended = with_halo(state, ((TILE, 2),), STEPS * CB)
    for _ in range(STEPS):
        extended = relax(extended)
    return extended


def on_device(members, vertical, jacobian, sketch_bits, test_bits, obs_column, obs_slot):
    tile_count = lax.axis_size(TILE)
    my_tile = lax.axis_index(TILE)
    obs_local = obs_column.shape[0]
    levels = members.shape[1]
    cell_count = members.shape[2]
    channels = jacobian.shape[1]
    capacity = obs_local // 4
    slot_count = tile_count * capacity
    ensemble = members.shape[0] * lax.axis_size("mem")
    count = float(obs_local * tile_count * channels)
    all_columns, all_slots = gather_turned((obs_column, obs_slot), TILE, (0, 0))
    owners = jnp.arange(tile_count * obs_local, dtype=jnp.int32) // obs_local
    target = jnp.where(
        all_columns // cell_count == my_tile, owners * capacity + all_slots, slot_count
    )
    cell_table = (
        jnp.zeros((slot_count,), jnp.int32).at[target].set(all_columns % cell_count, mode="drop")
    )
    occupied = jnp.zeros((slot_count,), jnp.bool_).at[target].set(True, mode="drop")
    spread = ((cell_table[:, None] == jnp.arange(cell_count)[None, :]) & occupied[:, None]).astype(
        jnp.bfloat16
    )
    my_positions = obs_column // cell_count * capacity + obs_slot
    collect = (my_positions[:, None] == jnp.arange(slot_count)[None, :]).astype(jnp.bfloat16)

    def apply_operator(vectors):
        probes = vectors.shape[0]
        rows = probes * levels
        adjoint = jnp.einsum(
            "ocl,poc->plo",
            jacobian,
            vectors.astype(jnp.bfloat16),
            preferred_element_type=jnp.float32,
        ).astype(jnp.bfloat16)
        outgoing = jnp.dot(
            adjoint.reshape(rows, obs_local), collect, preferred_element_type=jnp.float32
        ).astype(jnp.bfloat16)
        arrived = lax.all_to_all(outgoing, TILE, split_axis=1, concat_axis=1, tiled=True)
        field_sum = jnp.dot(arrived, spread, preferred_element_type=jnp.float32).reshape(
            probes, levels, cell_count
        )

        def member_step(number, carry):
            member = lax.dynamic_index_in_dim(members, number, 0, keepdims=False).astype(
                jnp.float32
            )
            product = (member[None] * field_sum).astype(jnp.bfloat16)
            mixed = jnp.einsum("kl,plc->pkc", vertical, product, preferred_element_type=jnp.float32)
            return carry + member[None] * diffuse(mixed)

        partial_sum = lax.fori_loop(
            0, members.shape[0], member_step, jnp.zeros((probes, levels, cell_count), jnp.float32)
        )
        partial_cols = jnp.take(partial_sum.reshape(rows, cell_count), cell_table, axis=1).reshape(
            rows, tile_count, capacity
        )
        picked = sum_at_owner(partial_cols, "mem", 2) / (ensemble - 1)
        outbound = picked.astype(jnp.bfloat16)
        returned = lax.all_to_all(outbound, TILE, split_axis=1, concat_axis=1, tiled=True)
        returned = collect_2(returned, "mem", 2)
        returned = returned.reshape(rows, slot_count)
        profile = jnp.dot(returned, collect.T, preferred_element_type=jnp.float32).astype(
            jnp.bfloat16
        )
        profile = profile.reshape(probes, levels, obs_local)
        return jnp.einsum("ocl,plo->poc", jacobian, profile, preferred_element_type=jnp.float32)

    sketch = (2 * sketch_bits - 1).astype(jnp.float32)
    test = (2 * test_bits - 1).astype(jnp.float32)
    sketch_image = apply_operator(sketch)
    products = by_axis(
        jnp.einsum("ioc,joc->ij", sketch_image, sketch_image, precision=highest), TILE
    )
    lower = jnp.linalg.cholesky(products)
    inverse_lower = lax.linalg.triangular_solve(
        lower, jnp.eye(K, dtype=jnp.float32), left_side=True, lower=True
    )
    basis = jnp.sqrt(count) * jnp.einsum(
        "ji,ioc->joc", inverse_lower, sketch_image, precision=highest
    )
    intersection = by_axis(jnp.einsum("ioc,joc->ij", basis, test, precision=highest), TILE) / count
    remainder = test - jnp.einsum("ij,ioc->joc", intersection, basis, precision=highest)
    images = apply_operator(jnp.concatenate([basis, remainder], axis=0))
    image_q = images[:K]
    image_w = images[K:]
    trace_q, trace_w = (
        by_axis(jnp.sum(basis * image_q), TILE),
        by_axis(jnp.sum(remainder * image_w), TILE),
    )
    trace_mean = trace_q / (count * count) + trace_w / (K * count)
    sketch_rayleigh = trace_q / (K * count)
    return (image_q, image_w, trace_mean, sketch_rayleigh)


def solution(mesh):
    finer = Mesh(mesh.devices.reshape(mesh.shape["mem"], 4, 4), ("mem", "tile_0", "tile_1"))
    return jax.shard_map(
        on_device,
        mesh=finer,
        in_specs=(
            P("mem", None, TILE),
            P(),
            P(TILE, None, None),
            P(None, TILE, None),
            P(None, TILE, None),
            P(TILE),
            P(TILE),
        ),
        out_specs=(P(None, TILE, None), P(None, TILE, None), P(), P()),
        check_vma=False,
    )
```

profile of v0, /device:TPU:0, one launch (start us, length us, event | category | flops | bytes accessed | tf_op | source)
XLA Modules:
  0.0 431.1 jit_solution(6855449706677383312)
XLA Ops:
  0.6 13.3 %copy.96 = bf16[128,231,137]{1,2,0:T(8,128)(2,1)} copy(bf16[128,231,137]{0,1,2:T(8,128)(2,1)} %param.13) | data formatting | bytes 16203264 | tf_op args[2]
  22.1 8.2 %all-to-all-start = ((bf16[411,16,32]{0,2,1:T(8,128)(2,1)}), bf16[411,16,32]{0,2,1:T(8,128)(2,1)S(1)}, u32[]{:S(2)}, u32[]{:S(2)}) async-start(bf16[411,16,32]{0,2,1:T(8,128)(2,1)} %bitcast.5), calls=%async_computation | async-start | bytes 1048576 | tf_op jit(solution)/shard_map/all_to_all | solution.py:138
  30.2 25.7 %all_gather.3 = s32[2048,2]{0,1:T(2,128)S(1)} all-gather(s32[128,2]{0,1:T(2,128)S(1)} %pad_add_fusion), channel_id=1, replica_groups=mesh['mem'=8,'tile_0'=4,'tile_1'=4] {'tile_0','tile_1'}, dimensions={0}, use_global_device_ids=true | all-gather | bytes 17408 | tf_op jit(solution)/shard_map/all_gather | solution.py:33
  56.1 8.0 %scatter_custom_fusion = s32[512]{0:T(512)S(1)} fusion(s32[2048]{0:T(1024)S(1)} %bitcast.110, s32[2048]{0:T(1024)S(1)} %add_select_fusion.12, s32[]{:T(128)} %constant.386.clone.1), kind=kCustom, calls=%fused_computation.340 | custom fusion | bytes 2052 | tf_op jit(solution)/shard_map/scatter | solution.py:117
  64.3 9.1 %scatter_custom_fusion.1 = pred[512]{0:T(512)(128)(4,1)S(1)} fusion(s32[2048]{0:T(1024)S(1)} %bitcast.111, pred[2048]{0:T(1024)(128)(4,1)S(1)} %broadcast.1456, pred[]{:T(512)} %constant.400.clone.1), kind=kCustom, calls=%fused_computation.342 | custom fusion | bytes 513 | tf_op jit(solution)/shard_map/scatter | solution.py:119
  77.0 49.0 %while.32 = (s32[]{:T(128)}, f32[3,137,512]{2,1,0:T(8,128)S(1)}, bf16[2,137,512]{2,1,0:T(8,128)(2,1)S(1)}, f32[3,137,512]{2,1,0:T(8,128)S(1)}, bf16[137,137]{1,0:T(8,128)(2,1)S(1)}, /*index=5*/s32[]{:T(128)}, s32[]{:T(128)}) while((s32[]{:T(128)}, f32[3,137,512]{2,1,0:T(8,128)S(1)}, bf16[2,137,512]{2,1,0:T(8,128)(2,1)S(1)}, ...), condition=%wide.region_3.4_spmd.clone, body=%wide.region_2.3_spmd.clone.sunk | while | flops 77786176 | bytes 52359552 | solution.py:151
  81.0 6.5 %collective-permute-done = f32[3,137,192]{2,1,0:T(8,128)} collective-permute-done((f32[3,137,192]{2,1,0:T(8,128)}, f32[3,137,192]{2,1,0:T(8,128)}, u32[]{:S(2)}, u32[]{:S(2)}) %collective-permute-start) | collective-permute-done | bytes 315680 | tf_op jit(solution)/shard_map/while/body/eval_jaxpr/ppermute | solution.py:24
  106.4 6.5 %collective-permute-done = f32[3,137,192]{2,1,0:T(8,128)} collective-permute-done((f32[3,137,192]{2,1,0:T(8,128)}, f32[3,137,192]{2,1,0:T(8,128)}, u32[]{:S(2)}, u32[]{:S(2)}) %collective-permute-start) | collective-permute-done | bytes 315680 | tf_op jit(solution)/shard_map/while/body/eval_jaxpr/ppermute | solution.py:24
  129.5 20.5 %all_to_all.48 = f32[8,411,16,4]{1,3,2,0:T(4,128)S(1)} all-to-all(f32[8,411,16,4]{1,3,2,0:T(4,128)S(1)} %copy.102), channel_id=1, replica_groups=mesh['mem'=8,'tile_0'=4,'tile_1'=4] {'mem'}, dimensions={0} | all-to-all | bytes 1683456 | tf_op jit(solution)/shard_map/all_to_all | solution.py:50
  150.3 10.2 %all_to_all.49 = bf16[411,16,4]{0,2,1:T(4,128)(2,1)S(1)} all-to-all(bf16[411,16,4]{0,2,1:T(4,128)(2,1)S(1)} %multiply_convert_fusion.5), channel_id=1, replica_groups=mesh['mem'=8,'tile_0'=4,'tile_1'=4] {'tile_0','tile_1'}, dimensions={1} | all-to-all | bytes 105216 | tf_op jit(solution)/shard_map/all_to_all | solution.py:159
  160.6 12.8 %all_to_all.50 = bf16[8,411,16,4]{1,3,2,0:T(4,128)(2,1)S(1)} all-to-all(bf16[8,411,16,4]{1,3,2,0:T(4,128)(2,1)S(1)} %broadcast_in_dim.146), channel_id=1, replica_groups=mesh['mem'=8,'tile_0'=4,'tile_1'=4] {'mem'}, dimensions={0} | all-to-all | bytes 841728 | tf_op jit(solution)/shard_map/all_to_all | solution.py:56
  182.0 8.8 %psum.56 = f32[3,3]{0,1:T(4,128)S(1)} all-reduce(f32[3,3]{0,1:T(4,128)S(1)} %convolution_bitcast_fusion.5), channel_id=1, replica_groups=mesh['mem'=8,'tile_0'=4,'tile_1'=4] {'tile_0'}, use_global_device_ids=true, to_apply=%region_5.6 | all-reduce | flops 9 | bytes 72 | tf_op jit(solution)/shard_map/psum | solution.py:74
  191.1 8.9 %psum.57 = f32[3,3]{0,1:T(4,128)S(1)} all-reduce(f32[3,3]{0,1:T(4,128)S(1)} %psum.56), channel_id=1, replica_groups=mesh['mem'=8,'tile_0'=4,'tile_1'=4] {'tile_1'}, use_global_device_ids=true, to_apply=%region_6.7 | all-reduce | flops 9 | bytes 72 | tf_op jit(solution)/shard_map/psum | solution.py:74
  205.4 8.6 %psum.58 = f32[3,3]{1,0:T(4,128)S(1)} all-reduce(f32[3,3]{1,0:T(4,128)S(1)} %convolution_bitcast_fusion.3), channel_id=1, replica_groups=mesh['mem'=8,'tile_0'=4,'tile_1'=4] {'tile_0'}, use_global_device_ids=true, to_apply=%region_9.10 | all-reduce | flops 9 | bytes 72 | tf_op jit(solution)/shard_map/psum | solution.py:74
  214.0 8.6 %psum.59 = f32[3,3]{1,0:T(4,128)S(1)} all-reduce(f32[3,3]{1,0:T(4,128)S(1)} %psum.58), channel_id=1, replica_groups=mesh['mem'=8,'tile_0'=4,'tile_1'=4] {'tile_1'}, use_global_device_ids=true, to_apply=%region_10.11 | all-reduce | flops 9 | bytes 72 | tf_op jit(solution)/shard_map/psum | solution.py:74
  236.3 12.4 %all-to-all-done.4 = bf16[822,16,32]{0,2,1:T(8,128)(2,1)S(1)} async-done(((bf16[822,16,32]{0,2,1:T(8,128)(2,1)}), bf16[822,16,32]{0,2,1:T(8,128)(2,1)S(1)}, u32[]{:S(2)}, u32[]{:S(2)}) %all-to-all-start.4) | async-done | bytes 841760 | tf_op jit(solution)/shard_map/all_to_all | solution.py:138
  255.6 79.9 %while.33 = (s32[]{:T(128)}, f32[6,137,512]{2,1,0:T(8,128)}, bf16[2,137,512]{2,1,0:T(8,128)(2,1)S(1)}, f32[6,137,512]{2,1,0:T(8,128)}, bf16[137,137]{1,0:T(8,128)(2,1)S(1)}, /*index=5*/s32[]{:T(128)}, s32[]{:T(128)}) while((s32[]{:T(128)}, f32[6,137,512]{2,1,0:T(8,128)}, bf16[2,137,512]{2,1,0:T(8,128)(2,1)S(1)}, ...), condition=%wide.region_12.13_spmd.clone, body=%wide.region_11.12_spmd.clone.sunk | while | flops 155461888 | bytes 112613240 | solution.py:151
  261.1 11.3 %collective-permute-done.2 = f32[6,137,192]{2,1,0:T(8,128)} collective-permute-done((f32[6,137,192]{2,1,0:T(8,128)}, f32[6,137,192]{2,1,0:T(8,128)}, u32[]{:S(2)}, u32[]{:S(2)}) %collective-permute-start.2) | collective-permute-done | bytes 631328 | tf_op jit(solution)/shard_map/while/body/eval_jaxpr/ppermute | solution.py:24
  301.4 11.3 %collective-permute-done.2 = f32[6,137,192]{2,1,0:T(8,128)} collective-permute-done((f32[6,137,192]{2,1,0:T(8,128)}, f32[6,137,192]{2,1,0:T(8,128)}, u32[]{:S(2)}, u32[]{:S(2)}) %collective-permute-start.2) | collective-permute-done | bytes 631328 | tf_op jit(solution)/shard_map/while/body/eval_jaxpr/ppermute | solution.py:24
  343.3 26.8 %all_to_all.51 = f32[8,822,16,4]{1,3,2,0:T(4,128)S(1)} all-to-all(f32[8,822,16,4]{1,3,2,0:T(4,128)S(1)} %copy.123), channel_id=1, replica_groups=mesh['mem'=8,'tile_0'=4,'tile_1'=4] {'mem'}, dimensions={0} | all-to-all | bytes 3366912 | tf_op jit(solution)/shard_map/all_to_all | solution.py:50
  370.6 10.5 %all_to_all.52 = bf16[822,16,4]{0,2,1:T(4,128)(2,1)S(1)} all-to-all(bf16[822,16,4]{0,2,1:T(4,128)(2,1)S(1)} %multiply_convert_fusion.4), channel_id=1, replica_groups=mesh['mem'=8,'tile_0'=4,'tile_1'=4] {'tile_0','tile_1'}, dimensions={1} | all-to-all | bytes 210432 | tf_op jit(solution)/shard_map/all_to_all | solution.py:159
  381.4 17.0 %all_to_all.53 = bf16[8,822,16,4]{1,3,2,0:T(4,128)(2,1)S(1)} all-to-all(bf16[8,822,16,4]{1,3,2,0:T(4,128)(2,1)S(1)} %broadcast_in_dim.148), channel_id=1, replica_groups=mesh['mem'=8,'tile_0'=4,'tile_1'=4] {'mem'}, dimensions={0} | all-to-all | bytes 1683456 | tf_op jit(solution)/shard_map/all_to_all | solution.py:56
  407.9 9.2 %all-reduce.1 = (f32[]{:T(128)}, f32[]{:T(128)}) all-reduce(f32[]{:T(128)} %get-tuple-element.418, f32[]{:T(128)} %get-tuple-element.384), channel_id=1, replica_groups=mesh['mem'=8,'tile_0'=4,'tile_1'=4] {'tile_0'}, use_global_device_ids=true, to_apply=%region_15.16 | all-reduce | flops 2 | bytes 16 | tf_op jit(solution)/shard_map/psum | solution.py:74
  417.1 9.6 %all-reduce = (f32[]{:T(128)}, f32[]{:T(128)}) all-reduce(f32[]{:T(128)} %get-tuple-element.382, f32[]{:T(128)} %get-tuple-element.383), channel_id=1, replica_groups=mesh['mem'=8,'tile_0'=4,'tile_1'=4] {'tile_1'}, use_global_device_ids=true, to_apply=%region_16.17 | all-reduce | flops 2 | bytes 16 | tf_op jit(solution)/shard_map/psum | solution.py:74
  (208 shorter events, 160.8 us)
Async XLA Ops:
  0.6 13.3 %copy-start.13 = (s32[3,128,231]{1,2,0:T(8,128)S(1)}, s32[3,128,231]{1,2,0:T(8,128)}, u32[]{:S(2)}) copy-start(s32[3,128,231]{1,2,0:T(8,128)} %param.14) | copy-start | bytes 1064452
  14.2 6.4 %copy-start.21 = (s32[128]{0:T(128)S(1)}, s32[128]{0:T(128)}, u32[]{:S(2)}) copy-start(s32[128]{0:T(128)} %param.17) | copy-start | bytes 1540
  14.2 6.4 %copy-start.22 = (s32[128]{0:T(128)S(1)}, s32[128]{0:T(128)}, u32[]{:S(2)}) copy-start(s32[128]{0:T(128)} %param.16) | copy-start | bytes 1540
  20.4 43.7 %copy-start.14 = (bf16[2,137,512]{2,0,1:T(2,128)(2,1)S(1)}, bf16[2,137,512]{2,0,1:T(2,128)(2,1)}, u32[]{:S(2)}) copy-start(bf16[2,137,512]{2,0,1:T(2,128)(2,1)} %param.11) | copy-start | bytes 841732
  20.7 210.2 %copy-start.19 = (s32[128]{0:T(128)}, s32[128]{0:T(128)S(1)}, u32[]{:S(2)}) copy-start(s32[128]{0:T(128)S(1)} %multiply_add_fusion) | copy-start | bytes 1540
  22.1 51.5 %all-to-all-start = ((bf16[411,16,32]{0,2,1:T(8,128)(2,1)}), bf16[411,16,32]{0,2,1:T(8,128)(2,1)S(1)}, u32[]{:S(2)}, u32[]{:S(2)}) async-start(bf16[411,16,32]{0,2,1:T(8,128)(2,1)} %bitcast.5), calls=%async_computation | async-start | bytes 1048576 | tf_op jit(solution)/shard_map/all_to_all | solution.py:138
  64.3 64.8 %copy-start.15 = (pred[16,8,4]{2,1,0:T(8,128)(4,1)}, pred[16,8,4]{2,1,0:T(8,128)(4,1)S(1)}, u32[]{:S(2)}) copy-start(pred[16,8,4]{2,1,0:T(8,128)(4,1)S(1)} %broadcast_in_dim.137) | copy-start | bytes 1540
  73.5 53.6 %copy-start.17 = (s32[1024]{0:T(1024)}, s32[1024]{0:T(1024)S(1)}, u32[]{:S(2)}) copy-start(s32[1024]{0:T(1024)S(1)} %pad_clamp_fusion) | copy-start | bytes 12292
  73.5 3.5 copy-start.8
  78.9 8.6 %collective-permute-start = (f32[3,137,192]{2,1,0:T(8,128)}, f32[3,137,192]{2,1,0:T(8,128)}, u32[]{:S(2)}, u32[]{:S(2)}) collective-permute-start(f32[3,137,192]{2,1,0:T(8,128)} %get-tuple-element.507), channel_id=1, source_target_pairs={{1,0},{2,1},{3,2},{4,3},{5,4},{6,5},{7,6},{8,7},{9,8},{10,9},{11,1... | collective-permute-start | bytes 946952 | tf_op jit(solution)/shard_map/while/body/eval_jaxpr/ppermute | solution.py:24
  81.0 11.7 %collective-permute-start.1 = (f32[3,137,192]{2,1,0:T(8,128)S(1)}, f32[3,137,192]{2,1,0:T(8,128)}, u32[]{:S(2)}, u32[]{:S(2)}) collective-permute-start(f32[3,137,192]{2,1,0:T(8,128)S(1)} %get-tuple-element.508), channel_id=1, source_target_pairs={{0,1},{1,2},{2,3},{3,4},{4,5},{5,6},{6,7},{7,8},{8,9},{9,10},{10,1... | collective-permute-start | bytes 946952 | tf_op jit(solution)/shard_map/while/body/eval_jaxpr/ppermute | solution.py:21
  104.3 8.6 %collective-permute-start = (f32[3,137,192]{2,1,0:T(8,128)}, f32[3,137,192]{2,1,0:T(8,128)}, u32[]{:S(2)}, u32[]{:S(2)}) collective-permute-start(f32[3,137,192]{2,1,0:T(8,128)} %get-tuple-element.507), channel_id=1, source_target_pairs={{1,0},{2,1},{3,2},{4,3},{5,4},{6,5},{7,6},{8,7},{9,8},{10,9},{11,1... | collective-permute-start | bytes 946952 | tf_op jit(solution)/shard_map/while/body/eval_jaxpr/ppermute | solution.py:24
  104.5 11.7 %collective-permute-start.1 = (f32[3,137,192]{2,1,0:T(8,128)S(1)}, f32[3,137,192]{2,1,0:T(8,128)}, u32[]{:S(2)}, u32[]{:S(2)}) collective-permute-start(f32[3,137,192]{2,1,0:T(8,128)S(1)} %get-tuple-element.508), channel_id=1, source_target_pairs={{0,1},{1,2},{2,3},{3,4},{4,5},{5,6},{6,7},{7,8},{8,9},{9,10},{10,1... | collective-permute-start | bytes 946952 | tf_op jit(solution)/shard_map/while/body/eval_jaxpr/ppermute | solution.py:21
  174.5 7.4 %copy-start.11 = (s32[3,128,231]{1,2,0:T(8,128)S(1)}, s32[3,128,231]{1,2,0:T(8,128)}, u32[]{:S(2)}) copy-start(s32[3,128,231]{1,2,0:T(8,128)} %param.15) | copy-start | bytes 1064452
  203.2 20.7 %copy-start.6 = (f32[3,128,231]{1,2,0:T(8,128)}, f32[3,128,231]{1,2,0:T(8,128)S(1)}, u32[]{:S(2)}) copy-start(f32[3,128,231]{1,2,0:T(8,128)S(1)} %get-tuple-element.389) | copy-start | bytes 1064452
  223.7 6.8 %copy-start.9 = (f32[3,128,231]{1,0,2:T(4,128)}, f32[3,128,231]{1,0,2:T(4,128)S(1)}, u32[]{:S(2)}) copy-start(f32[3,128,231]{1,0,2:T(4,128)S(1)} %fusion.190) | copy-start | bytes 1064452
  232.7 16.1 %all-to-all-start.4 = ((bf16[822,16,32]{0,2,1:T(8,128)(2,1)}), bf16[822,16,32]{0,2,1:T(8,128)(2,1)S(1)}, u32[]{:S(2)}, u32[]{:S(2)}) async-start(bf16[822,16,32]{0,2,1:T(8,128)(2,1)} %bitcast.19), calls=%async_computation.4 | async-start | bytes 1835008 | tf_op jit(solution)/shard_map/all_to_all | solution.py:138
  251.8 3.8 copy-start.5
  259.0 13.4 %collective-permute-start.2 = (f32[6,137,192]{2,1,0:T(8,128)}, f32[6,137,192]{2,1,0:T(8,128)}, u32[]{:S(2)}, u32[]{:S(2)}) collective-permute-start(f32[6,137,192]{2,1,0:T(8,128)} %get-tuple-element.526), channel_id=1, source_target_pairs={{1,0},{2,1},{3,2},{4,3},{5,4},{6,5},{7,6},{8,7},{9,8},{10,9},{11,1... | collective-permute-start | bytes 1893896 | tf_op jit(solution)/shard_map/while/body/eval_jaxpr/ppermute | solution.py:24
  260.2 16.5 %collective-permute-start.3 = (f32[6,137,192]{2,1,0:T(8,128)S(1)}, f32[6,137,192]{2,1,0:T(8,128)}, u32[]{:S(2)}, u32[]{:S(2)}) collective-permute-start(f32[6,137,192]{2,1,0:T(8,128)S(1)} %get-tuple-element.527), channel_id=1, source_target_pairs={{0,1},{1,2},{2,3},{3,4},{4,5},{5,6},{6,7},{7,8},{8,9},{9,10},{10,1... | collective-permute-start | bytes 1893896 | tf_op jit(solution)/shard_map/while/body/eval_jaxpr/ppermute | solution.py:21
  290.4 2.4 copy-start
  299.3 13.4 %collective-permute-start.2 = (f32[6,137,192]{2,1,0:T(8,128)}, f32[6,137,192]{2,1,0:T(8,128)}, u32[]{:S(2)}, u32[]{:S(2)}) collective-permute-start(f32[6,137,192]{2,1,0:T(8,128)} %get-tuple-element.526), channel_id=1, source_target_pairs={{1,0},{2,1},{3,2},{4,3},{5,4},{6,5},{7,6},{8,7},{9,8},{10,9},{11,1... | collective-permute-start | bytes 1893896 | tf_op jit(solution)/shard_map/while/body/eval_jaxpr/ppermute | solution.py:24
  299.5 16.5 %collective-permute-start.3 = (f32[6,137,192]{2,1,0:T(8,128)S(1)}, f32[6,137,192]{2,1,0:T(8,128)}, u32[]{:S(2)}, u32[]{:S(2)}) collective-permute-start(f32[6,137,192]{2,1,0:T(8,128)S(1)} %get-tuple-element.527), channel_id=1, source_target_pairs={{0,1},{1,2},{2,3},{3,4},{4,5},{5,6},{6,7},{7,8},{8,9},{9,10},{10,1... | collective-permute-start | bytes 1893896 | tf_op jit(solution)/shard_map/while/body/eval_jaxpr/ppermute | solution.py:21
  329.6 2.4 copy-start
  (13 other events, 13.5 us)
where the time goes:
time: 439 us; the launch traced here: 431 us
  blocking collectives  177 us (40%)
  waiting for transfers between devices  64.1 us (15%)
  local copies, waits for them, and re-layouts  61.2 us (14%)
  other arithmetic  60.9 us (14%)
  matrix products  41.2 us (9%)
  starting transfers between devices  19.9 us (5%)
  between operations  5.68 us (1%)
    psum x6, blocking collectives, by_axis(): value = lax.psum(value, axis)  53.8 us
    all_to_all x2, blocking collectives, sum_at_owner(): lax.all_to_all(pieces, axis, split_axis=0, concat_axis=0, tiled=True)  47.3 us
    add x20, other arithmetic, relax(): center + diffusion_rate * (north - center + (south - center) + west_ok *...  41.3 us
    ppermute x4, waiting for transfers between devices, with_halo(): lax.ppermute(lax.slice_in_dim(block, 0, width, axis=dim), axis, backward)  35.6 us
    all_to_all x2, blocking collectives, from_everyone(): lax.all_to_all(jnp.broadcast_to(value[None], (peers, *value.shape)), axis...  29.7 us
    all_gather x1, blocking collectives, gather_turned(): whole = lax.all_gather(both, axis, axis=0, tiled=True)  25.7 us
    all_to_all x2, blocking collectives, apply_operator(): lax.all_to_all(outbound, TILE, split_axis=1, concat_axis=1, tiled=True)  20.7 us
    ppermute x4, waiting for transfers between devices, with_halo(): lax.ppermute(lax.slice_in_dim(block, block.shape[dim] - width, None, axis...  16.1 us
  transfers between devices with their start and end apart: 10, of which 9 were waited for; matrix products, arithmetic and copies ran while one was open for 4% of the time, Pallas kernels for 0%

commit v1 on v0

--- a/solution.py
+++ b/solution.py
@@ -10,6 +10,12 @@
 TILE = ("tile_0", "tile_1")
 diffusion_rate = 0.2
 highest = lax.Precision.HIGHEST
+
+
+def summed_here(shard, name):
+    parts = lax.all_gather(shard, name, axis=0, tiled=False)
+    total = parts.sum(axis=0)
+    return total
 
 
 def with_halo(block, sides, width):
@@ -71,7 +77,7 @@
 
 def by_axis(value, axes):
     for axis in axes:
-        value = lax.psum(value, axis)
+        value = summed_here(value, axis)
     return value
 
 

time: 439 us -> 460 us (1.048)
  blocking collectives: 177 us -> 133 us
  waiting for transfers between devices: 64.1 us -> 104 us
  starting transfers between devices: 19.9 us -> 33.5 us
  local copies, waits for them, and re-layouts: 61.2 us -> 70.7 us
    psum x6 -> x0, blocking collectives: 53.8 us -> none  [by_axis(): value = lax.psum(value, axis)]
    all_gather x0 -> x4, blocking collectives: none -> 42 us  [summed_here(): parts = lax.all_gather(shard, name, axis=0, tiled=False)]
    all_to_all x0 -> x3, waiting for transfers between devices: none -> 39.9 us  [the longest x2 24 us: from_everyone(): lax.all_to_all(jnp.broadcast_to(value[None], (peers, *value.shape)), axis...]
    all_to_all x2 -> x0, blocking collectives: 29.7 us -> none  [from_everyone(): lax.all_to_all(jnp.broadcast_to(value[None], (peers, *value.shape)), axis...]
    all_to_all x2 -> x1, blocking collectives: 47.3 us -> 26.8 us  [sum_at_owner(): lax.all_to_all(pieces, axis, split_axis=0, concat_axis=0, tiled=True)]
    unnamed x0 -> x2, blocking collectives: none -> 17.5 us
    all_to_all x0 -> x3, starting transfers between devices: none -> 11.7 us  [the longest x2 7.04 us: from_everyone(): lax.all_to_all(jnp.broadcast_to(value[None], (peers, *value.shape)), axis...]
    unnamed x40 -> x54, local copies, waits for them, and re-layouts: 15 us -> 21.7 us
  transfers between devices with their start and end apart: 10 -> 13, of which waited for: 9 -> 12; matrix products, arithmetic and copies ran while one was open for 4% -> 4% of each run, Pallas kernels for 0% -> 0%
where the time goes in v1:
time: 460 us; the launch traced here: 452 us
  blocking collectives  133 us (29%)
  waiting for transfers between devices  104 us (23%)
  local copies, waits for them, and re-layouts  70.7 us (15%)
  other arithmetic  63.5 us (14%)
  matrix products  41.1 us (9%)
  starting transfers between devices  33.5 us (7%)
  between operations  5.75 us (1%)
    all_gather x4, blocking collectives, summed_here(): parts = lax.all_gather(shard, name, axis=0, tiled=False)  42 us
    add x20, other arithmetic, relax(): center + diffusion_rate * (north - center + (south - center) + west_ok *...  41.3 us
    ppermute x4, waiting for transfers between devices, with_halo(): lax.ppermute(lax.slice_in_dim(block, 0, width, axis=dim), axis, backward)  35.6 us
    all_to_all x1, blocking collectives, sum_at_owner(): lax.all_to_all(pieces, axis, split_axis=0, concat_axis=0, tiled=True)  26.8 us
    all_gather x1, blocking collectives, gather_turned(): whole = lax.all_gather(both, axis, axis=0, tiled=True)  25.7 us
    all_to_all x2, waiting for transfers between devices, from_everyone(): lax.all_to_all(jnp.broadcast_to(value[None], (peers, *value.shape)), axis...  24 us
    unnamed x54, local copies, waits for them, and re-layouts  21.7 us
    all_to_all x2, blocking collectives, apply_operator(): lax.all_to_all(outbound, TILE, split_axis=1, concat_axis=1, tiled=True)  20.7 us
  transfers between devices with their start and end apart: 13, of which 12 were waited for; matrix products, arithmetic and copies ran while one was open for 4% of the time, Pallas kernels for 0%

profile of v1, /device:TPU:0, one launch (start us, length us, event | category | flops | bytes accessed | tf_op | source)
XLA Modules:
  0.0 452.2 jit_solution(10291996706908958864)
XLA Ops:
  0.6 13.2 %copy.93 = bf16[128,231,137]{1,2,0:T(8,128)(2,1)} copy(bf16[128,231,137]{0,1,2:T(8,128)(2,1)} %param.13) | data formatting | bytes 16203264 | tf_op args[2]
  22.0 8.2 %all-to-all-start = ((bf16[411,16,32]{0,2,1:T(8,128)(2,1)}), bf16[411,16,32]{0,2,1:T(8,128)(2,1)S(1)}, u32[]{:S(2)}, u32[]{:S(2)}) async-start(bf16[411,16,32]{0,2,1:T(8,128)(2,1)} %bitcast.5), calls=%async_computation | async-start | bytes 1048576 | tf_op jit(solution)/shard_map/all_to_all | solution.py:144
  30.2 25.7 %all_gather.51 = s32[2048,2]{0,1:T(2,128)S(1)} all-gather(s32[128,2]{0,1:T(2,128)S(1)} %pad_add_fusion), channel_id=1, replica_groups=mesh['mem'=8,'tile_0'=4,'tile_1'=4] {'tile_0','tile_1'}, dimensions={0}, use_global_device_ids=true | all-gather | bytes 17408 | tf_op jit(solution)/shard_map/all_gather | solution.py:39
  56.0 8.0 %scatter_custom_fusion = s32[512]{0:T(512)S(1)} fusion(s32[2048]{0:T(1024)S(1)} %bitcast.122, s32[2048]{0:T(1024)S(1)} %add_select_fusion.12, s32[]{:T(128)} %constant.386.clone.1), kind=kCustom, calls=%fused_computation.340 | custom fusion | bytes 2052 | tf_op jit(solution)/shard_map/scatter | solution.py:123
  64.2 9.1 %scatter_custom_fusion.1 = pred[512]{0:T(512)(128)(4,1)S(1)} fusion(s32[2048]{0:T(1024)S(1)} %bitcast.123, pred[2048]{0:T(1024)(128)(4,1)S(1)} %broadcast.1456, pred[]{:T(512)} %constant.400.clone.1), kind=kCustom, calls=%fused_computation.342 | custom fusion | bytes 513 | tf_op jit(solution)/shard_map/scatter | solution.py:125
  76.9 48.9 %while.32 = (s32[]{:T(128)}, f32[3,137,512]{2,1,0:T(8,128)S(1)}, bf16[2,137,512]{2,1,0:T(8,128)(2,1)S(1)}, f32[3,137,512]{2,1,0:T(8,128)S(1)}, bf16[137,137]{1,0:T(8,128)(2,1)S(1)}, /*index=5*/s32[]{:T(128)}, s32[]{:T(128)}) while((s32[]{:T(128)}, f32[3,137,512]{2,1,0:T(8,128)S(1)}, bf16[2,137,512]{2,1,0:T(8,128)(2,1)S(1)}, ...), condition=%wide.region_3.4_spmd.clone, body=%wide.region_2.3_spmd.clone.sunk | while | flops 77786176 | bytes 52359552 | solution.py:157
  80.9 6.5 %collective-permute-done = f32[3,137,192]{2,1,0:T(8,128)} collective-permute-done((f32[3,137,192]{2,1,0:T(8,128)}, f32[3,137,192]{2,1,0:T(8,128)}, u32[]{:S(2)}, u32[]{:S(2)}) %collective-permute-start) | collective-permute-done | bytes 315680 | tf_op jit(solution)/shard_map/while/body/eval_jaxpr/ppermute | solution.py:30
  106.3 6.5 %collective-permute-done = f32[3,137,192]{2,1,0:T(8,128)} collective-permute-done((f32[3,137,192]{2,1,0:T(8,128)}, f32[3,137,192]{2,1,0:T(8,128)}, u32[]{:S(2)}, u32[]{:S(2)}) %collective-permute-start) | collective-permute-done | bytes 315680 | tf_op jit(solution)/shard_map/while/body/eval_jaxpr/ppermute | solution.py:30
  135.1 15.9 %all-to-all-done.1 = f32[8,411,16,4]{1,3,2,0:T(4,128)S(1)} async-done(((f32[8,411,16,4]{1,3,2,0:T(4,128)}), f32[8,411,16,4]{1,3,2,0:T(4,128)S(1)}, u32[]{:S(2)}, u32[]{:S(2)}) %all-to-all-start.1) | async-done | bytes 841760 | tf_op jit(solution)/shard_map/all_to_all | solution.py:56
  151.3 10.2 %all_to_all.48 = bf16[411,16,4]{0,2,1:T(4,128)(2,1)S(1)} all-to-all(bf16[411,16,4]{0,2,1:T(4,128)(2,1)S(1)} %multiply_convert_fusion.5), channel_id=1, replica_groups=mesh['mem'=8,'tile_0'=4,'tile_1'=4] {'tile_0','tile_1'}, dimensions={1} | all-to-all | bytes 105216 | tf_op jit(solution)/shard_map/all_to_all | solution.py:165
  166.0 10.2 %all-to-all-done.3 = bf16[8,411,16,4]{1,3,2,0:T(4,128)(2,1)S(1)} async-done(((bf16[8,411,16,4]{1,3,2,0:T(4,128)(2,1)}), bf16[8,411,16,4]{1,3,2,0:T(4,128)(2,1)S(1)}, u32[]{:S(2)}, u32[]{:S(2)}) %all-to-all-start.3) | async-done | bytes 420896 | tf_op jit(solution)/shard_map/all_to_all | solution.py:62
  184.9 10.4 %all-gather.4 = f32[4,3,3]{2,1,0:T(4,128)S(1)} all-gather(f32[1,3,3]{2,1,0:T(4,128)S(1)} %convolution_bitcast_fusion.5), channel_id=2, replica_groups=mesh['mem'=8,'tile_0'=4,'tile_1'=4] {'tile_0'}, dimensions={0}, use_global_device_ids=true | all-gather | bytes 180 | tf_op jit(solution)/shard_map/all_gather | solution.py:16
  195.4 10.4 %all-gather.5 = f32[4,3,3]{2,1,0:T(4,128)S(1)} all-gather(f32[1,3,3]{2,1,0:T(4,128)S(1)} %bitcast.120), channel_id=3, replica_groups=mesh['mem'=8,'tile_0'=4,'tile_1'=4] {'tile_1'}, dimensions={0}, use_global_device_ids=true | all-gather | bytes 180 | tf_op jit(solution)/shard_map/all_gather | solution.py:16
  211.2 10.6 %all-gather.6 = f32[4,3,3]{2,1,0:T(4,128)S(1)} all-gather(f32[1,3,3]{2,1,0:T(4,128)S(1)} %convolution_bitcast_fusion.3), channel_id=4, replica_groups=mesh['mem'=8,'tile_0'=4,'tile_1'=4] {'tile_0'}, dimensions={0}, use_global_device_ids=true | all-gather | bytes 180 | tf_op jit(solution)/shard_map/all_gather | solution.py:16
  221.8 10.6 %all-gather.7 = f32[4,3,3]{2,1,0:T(4,128)S(1)} all-gather(f32[1,3,3]{2,1,0:T(4,128)S(1)} %bitcast.121), channel_id=5, replica_groups=mesh['mem'=8,'tile_0'=4,'tile_1'=4] {'tile_1'}, dimensions={0}, use_global_device_ids=true | all-gather | bytes 180 | tf_op jit(solution)/shard_map/all_gather | solution.py:16
  247.9 12.5 %all-to-all-done.4 = bf16[822,16,32]{0,2,1:T(8,128)(2,1)S(1)} async-done(((bf16[822,16,32]{0,2,1:T(8,128)(2,1)}), bf16[822,16,32]{0,2,1:T(8,128)(2,1)S(1)}, u32[]{:S(2)}, u32[]{:S(2)}) %all-to-all-start.4) | async-done | bytes 841760 | tf_op jit(solution)/shard_map/all_to_all | solution.py:144
  267.3 79.9 %while.33 = (s32[]{:T(128)}, f32[6,137,512]{2,1,0:T(8,128)}, bf16[2,137,512]{2,1,0:T(8,128)(2,1)S(1)}, f32[6,137,512]{2,1,0:T(8,128)}, bf16[137,137]{1,0:T(8,128)(2,1)S(1)}, /*index=5*/s32[]{:T(128)}, s32[]{:T(128)}) while((s32[]{:T(128)}, f32[6,137,512]{2,1,0:T(8,128)}, bf16[2,137,512]{2,1,0:T(8,128)(2,1)S(1)}, ...), condition=%wide.region_12.13_spmd.clone, body=%wide.region_11.12_spmd.clone.sunk | while | flops 155461888 | bytes 112613240 | solution.py:157
  272.7 11.3 %collective-permute-done.2 = f32[6,137,192]{2,1,0:T(8,128)} collective-permute-done((f32[6,137,192]{2,1,0:T(8,128)}, f32[6,137,192]{2,1,0:T(8,128)}, u32[]{:S(2)}, u32[]{:S(2)}) %collective-permute-start.2) | collective-permute-done | bytes 631328 | tf_op jit(solution)/shard_map/while/body/eval_jaxpr/ppermute | solution.py:30
  313.0 11.3 %collective-permute-done.2 = f32[6,137,192]{2,1,0:T(8,128)} collective-permute-done((f32[6,137,192]{2,1,0:T(8,128)}, f32[6,137,192]{2,1,0:T(8,128)}, u32[]{:S(2)}, u32[]{:S(2)}) %collective-permute-start.2) | collective-permute-done | bytes 631328 | tf_op jit(solution)/shard_map/while/body/eval_jaxpr/ppermute | solution.py:30
  355.0 26.8 %all_to_all.50 = f32[8,822,16,4]{1,3,2,0:T(4,128)S(1)} all-to-all(f32[8,822,16,4]{1,3,2,0:T(4,128)S(1)} %copy.119), channel_id=1, replica_groups=mesh['mem'=8,'tile_0'=4,'tile_1'=4] {'mem'}, dimensions={0} | all-to-all | bytes 3366912 | tf_op jit(solution)/shard_map/all_to_all | solution.py:56
  382.3 10.5 %all_to_all.49 = bf16[822,16,4]{0,2,1:T(4,128)(2,1)S(1)} all-to-all(bf16[822,16,4]{0,2,1:T(4,128)(2,1)S(1)} %multiply_convert_fusion.4), channel_id=1, replica_groups=mesh['mem'=8,'tile_0'=4,'tile_1'=4] {'tile_0','tile_1'}, dimensions={1} | all-to-all | bytes 210432 | tf_op jit(solution)/shard_map/all_to_all | solution.py:165
  398.2 13.8 %all-to-all-done.7 = bf16[8,822,16,4]{1,3,2,0:T(4,128)(2,1)S(1)} async-done(((bf16[8,822,16,4]{1,3,2,0:T(4,128)(2,1)}), bf16[8,822,16,4]{1,3,2,0:T(4,128)(2,1)S(1)}, u32[]{:S(2)}, u32[]{:S(2)}) %all-to-all-start.7) | async-done | bytes 841760 | tf_op jit(solution)/shard_map/all_to_all | solution.py:62
  424.9 8.6 %all-reduce.5 = (f32[4]{0:T(128)S(1)}, f32[4]{0:T(128)S(1)}) all-reduce(f32[4]{0:T(128)S(1)} %dynamic-update-slice.3, f32[4]{0:T(128)S(1)} %dynamic-update-slice.5), channel_id=1, replica_groups=mesh['mem'=8,'tile_0'=4,'tile_1'=4] {'tile_0'}, use_global_device_ids=true, to_apply=%add | all-reduce | flops 8 | bytes 64
  437.6 8.9 %all-reduce.4 = (f32[4]{0:T(128)S(1)}, f32[4]{0:T(128)S(1)}) all-reduce(f32[4]{0:T(128)S(1)} %dynamic-update-slice.4, f32[4]{0:T(128)S(1)} %dynamic-update-slice.6), channel_id=1, replica_groups=mesh['mem'=8,'tile_0'=4,'tile_1'=4] {'tile_1'}, use_global_device_ids=true, to_apply=%add.1 | all-reduce | flops 8 | bytes 64
  (233 shorter events, 186.3 us)
Async XLA Ops:
  0.6 13.2 %copy-start.13 = (s32[3,128,231]{1,2,0:T(8,128)S(1)}, s32[3,128,231]{1,2,0:T(8,128)}, u32[]{:S(2)}) copy-start(s32[3,128,231]{1,2,0:T(8,128)} %param.14) | copy-start | bytes 1064452
  14.1 6.4 %copy-start.21 = (s32[128]{0:T(128)S(1)}, s32[128]{0:T(128)}, u32[]{:S(2)}) copy-start(s32[128]{0:T(128)} %param.17) | copy-start | bytes 1540
  14.1 6.4 %copy-start.22 = (s32[128]{0:T(128)S(1)}, s32[128]{0:T(128)}, u32[]{:S(2)}) copy-start(s32[128]{0:T(128)} %param.16) | copy-start | bytes 1540
  20.4 43.7 %copy-start.14 = (bf16[2,137,512]{2,0,1:T(2,128)(2,1)S(1)}, bf16[2,137,512]{2,0,1:T(2,128)(2,1)}, u32[]{:S(2)}) copy-start(bf16[2,137,512]{2,0,1:T(2,128)(2,1)} %param.11) | copy-start | bytes 841732
  20.6 220.1 %copy-start.19 = (s32[128]{0:T(128)}, s32[128]{0:T(128)S(1)}, u32[]{:S(2)}) copy-start(s32[128]{0:T(128)S(1)} %multiply_add_fusion) | copy-start | bytes 1540
  22.0 51.5 %all-to-all-start = ((bf16[411,16,32]{0,2,1:T(8,128)(2,1)}), bf16[411,16,32]{0,2,1:T(8,128)(2,1)S(1)}, u32[]{:S(2)}, u32[]{:S(2)}) async-start(bf16[411,16,32]{0,2,1:T(8,128)(2,1)} %bitcast.5), calls=%async_computation | async-start | bytes 1048576 | tf_op jit(solution)/shard_map/all_to_all | solution.py:144
  64.2 64.8 %copy-start.15 = (pred[16,8,4]{2,1,0:T(8,128)(4,1)}, pred[16,8,4]{2,1,0:T(8,128)(4,1)S(1)}, u32[]{:S(2)}) copy-start(pred[16,8,4]{2,1,0:T(8,128)(4,1)S(1)} %broadcast_in_dim.137) | copy-start | bytes 1540
  73.4 53.6 %copy-start.17 = (s32[1024]{0:T(1024)}, s32[1024]{0:T(1024)S(1)}, u32[]{:S(2)}) copy-start(s32[1024]{0:T(1024)S(1)} %pad_clamp_fusion) | copy-start | bytes 12292
  78.8 8.6 %collective-permute-start = (f32[3,137,192]{2,1,0:T(8,128)}, f32[3,137,192]{2,1,0:T(8,128)}, u32[]{:S(2)}, u32[]{:S(2)}) collective-permute-start(f32[3,137,192]{2,1,0:T(8,128)} %get-tuple-element.507), channel_id=1, source_target_pairs={{1,0},{2,1},{3,2},{4,3},{5,4},{6,5},{7,6},{8,7},{9,8},{10,9},{11,1... | collective-permute-start | bytes 946952 | tf_op jit(solution)/shard_map/while/body/eval_jaxpr/ppermute | solution.py:30
  80.9 11.7 %collective-permute-start.1 = (f32[3,137,192]{2,1,0:T(8,128)S(1)}, f32[3,137,192]{2,1,0:T(8,128)}, u32[]{:S(2)}, u32[]{:S(2)}) collective-permute-start(f32[3,137,192]{2,1,0:T(8,128)S(1)} %get-tuple-element.508), channel_id=1, source_target_pairs={{0,1},{1,2},{2,3},{3,4},{4,5},{5,6},{6,7},{7,8},{8,9},{9,10},{10,1... | collective-permute-start | bytes 946952 | tf_op jit(solution)/shard_map/while/body/eval_jaxpr/ppermute | solution.py:27
  104.2 8.6 %collective-permute-start = (f32[3,137,192]{2,1,0:T(8,128)}, f32[3,137,192]{2,1,0:T(8,128)}, u32[]{:S(2)}, u32[]{:S(2)}) collective-permute-start(f32[3,137,192]{2,1,0:T(8,128)} %get-tuple-element.507), channel_id=1, source_target_pairs={{1,0},{2,1},{3,2},{4,3},{5,4},{6,5},{7,6},{8,7},{9,8},{10,9},{11,1... | collective-permute-start | bytes 946952 | tf_op jit(solution)/shard_map/while/body/eval_jaxpr/ppermute | solution.py:30
  104.4 11.7 %collective-permute-start.1 = (f32[3,137,192]{2,1,0:T(8,128)S(1)}, f32[3,137,192]{2,1,0:T(8,128)}, u32[]{:S(2)}, u32[]{:S(2)}) collective-permute-start(f32[3,137,192]{2,1,0:T(8,128)S(1)} %get-tuple-element.508), channel_id=1, source_target_pairs={{0,1},{1,2},{2,3},{3,4},{4,5},{5,6},{6,7},{7,8},{8,9},{9,10},{10,1... | collective-permute-start | bytes 946952 | tf_op jit(solution)/shard_map/while/body/eval_jaxpr/ppermute | solution.py:27
  130.4 20.6 %all-to-all-start.1 = ((f32[8,411,16,4]{1,3,2,0:T(4,128)}), f32[8,411,16,4]{1,3,2,0:T(4,128)S(1)}, u32[]{:S(2)}, u32[]{:S(2)}) async-start(f32[8,411,16,4]{1,3,2,0:T(4,128)} %copy.99), calls=%async_computation.1 | async-start | bytes 2097152 | tf_op jit(solution)/shard_map/all_to_all | solution.py:56
  135.1 30.9 %copy-start.11 = (s32[3,128,231]{1,2,0:T(8,128)S(1)}, s32[3,128,231]{1,2,0:T(8,128)}, u32[]{:S(2)}) copy-start(s32[3,128,231]{1,2,0:T(8,128)} %param.15) | copy-start | bytes 1064452
  162.4 13.7 %all-to-all-start.3 = ((bf16[8,411,16,4]{1,3,2,0:T(4,128)(2,1)}), bf16[8,411,16,4]{1,3,2,0:T(4,128)(2,1)S(1)}, u32[]{:S(2)}, u32[]{:S(2)}) async-start(bf16[8,411,16,4]{1,3,2,0:T(4,128)(2,1)} %broadcast_in_dim.146), calls=%async_computation.3 | async-start | bytes 1048576 | tf_op jit(solution)/shard_map/all_to_all | solution.py:62
  209.0 24.7 %copy-start.6 = (f32[3,128,231]{1,2,0:T(8,128)}, f32[3,128,231]{1,2,0:T(8,128)S(1)}, u32[]{:S(2)}) copy-start(f32[3,128,231]{1,2,0:T(8,128)S(1)} %get-tuple-element.389) | copy-start | bytes 1064452
  233.5 6.8 %copy-start.9 = (f32[3,128,231]{1,0,2:T(4,128)}, f32[3,128,231]{1,0,2:T(4,128)S(1)}, u32[]{:S(2)}) copy-start(f32[3,128,231]{1,0,2:T(4,128)S(1)} %fusion.190) | copy-start | bytes 1064452
  242.5 17.9 %all-to-all-start.4 = ((bf16[822,16,32]{0,2,1:T(8,128)(2,1)}), bf16[822,16,32]{0,2,1:T(8,128)(2,1)S(1)}, u32[]{:S(2)}, u32[]{:S(2)}) async-start(bf16[822,16,32]{0,2,1:T(8,128)(2,1)} %bitcast.23), calls=%async_computation.4 | async-start | bytes 1835008 | tf_op jit(solution)/shard_map/all_to_all | solution.py:144
  270.7 13.4 %collective-permute-start.2 = (f32[6,137,192]{2,1,0:T(8,128)}, f32[6,137,192]{2,1,0:T(8,128)}, u32[]{:S(2)}, u32[]{:S(2)}) collective-permute-start(f32[6,137,192]{2,1,0:T(8,128)} %get-tuple-element.526), channel_id=1, source_target_pairs={{1,0},{2,1},{3,2},{4,3},{5,4},{6,5},{7,6},{8,7},{9,8},{10,9},{11,1... | collective-permute-start | bytes 1893896 | tf_op jit(solution)/shard_map/while/body/eval_jaxpr/ppermute | solution.py:30
  271.9 16.5 %collective-permute-start.3 = (f32[6,137,192]{2,1,0:T(8,128)S(1)}, f32[6,137,192]{2,1,0:T(8,128)}, u32[]{:S(2)}, u32[]{:S(2)}) collective-permute-start(f32[6,137,192]{2,1,0:T(8,128)S(1)} %get-tuple-element.527), channel_id=1, source_target_pairs={{0,1},{1,2},{2,3},{3,4},{4,5},{5,6},{6,7},{7,8},{8,9},{9,10},{10,1... | collective-permute-start | bytes 1893896 | tf_op jit(solution)/shard_map/while/body/eval_jaxpr/ppermute | solution.py:27
  310.9 13.4 %collective-permute-start.2 = (f32[6,137,192]{2,1,0:T(8,128)}, f32[6,137,192]{2,1,0:T(8,128)}, u32[]{:S(2)}, u32[]{:S(2)}) collective-permute-start(f32[6,137,192]{2,1,0:T(8,128)} %get-tuple-element.526), channel_id=1, source_target_pairs={{1,0},{2,1},{3,2},{4,3},{5,4},{6,5},{7,6},{8,7},{9,8},{10,9},{11,1... | collective-permute-start | bytes 1893896 | tf_op jit(solution)/shard_map/while/body/eval_jaxpr/ppermute | solution.py:30
  311.1 16.5 %collective-permute-start.3 = (f32[6,137,192]{2,1,0:T(8,128)S(1)}, f32[6,137,192]{2,1,0:T(8,128)}, u32[]{:S(2)}, u32[]{:S(2)}) collective-permute-start(f32[6,137,192]{2,1,0:T(8,128)S(1)} %get-tuple-element.527), channel_id=1, source_target_pairs={{0,1},{1,2},{2,3},{3,4},{4,5},{5,6},{6,7},{7,8},{8,9},{9,10},{10,1... | collective-permute-start | bytes 1893896 | tf_op jit(solution)/shard_map/while/body/eval_jaxpr/ppermute | solution.py:27
  382.2 15.3 %copy-start.24 = (u32[128]{0:T(128)S(1)}, u32[128]{0:T(128)}, u32[]{:S(2)}) copy-start(u32[128]{0:T(128)} %constant.412) | copy-start | bytes 1540
  394.0 18.0 %all-to-all-start.7 = ((bf16[8,822,16,4]{1,3,2,0:T(4,128)(2,1)}), bf16[8,822,16,4]{1,3,2,0:T(4,128)(2,1)S(1)}, u32[]{:S(2)}, u32[]{:S(2)}) async-start(bf16[8,822,16,4]{1,3,2,0:T(4,128)(2,1)} %broadcast_in_dim.148), calls=%async_computation.7 | async-start | bytes 1835008 | tf_op jit(solution)/shard_map/all_to_all | solution.py:62
  (18 other events, 31.1 us)
